TPU v7x, 32 devices: a whole 2x2x4 slice. The times are simulated.
32 devices in a mesh: dp: 4 (over x, core), section: 2 (over y), tensor: 4 (over z).
Axes of the slice: x: 2, y: 2, z: 4, core: 2. Of those that a mesh axis runs over, the one named last changes fastest.
Arguments:
- section_input: bfloat16 [2, 512, 3072], P('section', 'dp'), may hold values from -6 to 6
- norm_gain: float32 [2, 3072], P('section'), may hold values from 0.25 to 1.75
- value_weight: bfloat16 [2, 1536, 3072], P('section', 'tensor'), may hold values from -0.109375 to 0.109375
- attn_probs: bfloat16 [2, 12, 512, 128], P('section', 'tensor', 'dp'), may hold values from 0 to 1, as said below
- out_weight: bfloat16 [2, 3072, 1536], P('section', None, 'tensor'), may hold values from -0.15625 to 0.15625
- direction: bfloat16 [2, 3072, 1536], P('section', None, 'tensor'), may hold values from -0.15625 to 0.15625
- curvature: bfloat16 [512, 3072], P('dp'), may hold values from 0.19921875 to 2
Outputs:
- curvature_product: float32 [2, 3072, 1536], P('section', 'dp', 'tensor')
Inputs may be any that keep to these rules, and one draw needn't show every extreme that they name: `attn_probs`: each row is a causal attention distribution over the 128 tokens of its sequence: nonnegative, summing to one up to rounding, zero for keys after the query's position in the sequence.
All inputs are finite; a program needn't handle non-finite values.
Results may differ from a plain program's by a relative error of at most 0.013.
Values may be sent and summed in bfloat16 or wider, within the bound.
A program may use at most 64 MiB of HBM per device.

v0:
```python
import jax
import jax.numpy as jnp
from jax import lax
from jax.sharding import PartitionSpec as P


def from_behind(block, axis, distance):
    devices = range(lax.axis_size(axis))
    route = [(i - distance, i) for i in devices if i - distance in devices]
    return lax.ppermute(block, axis, route)


def contract_last(left, right):
    return lax.dot_general(
        left, right, (((1,), (1,)), ((), ())), preferred_element_type=jnp.float32
    )


def contract_first(left, right):
    return lax.dot_general(
        left, right, (((0,), (0,)), ((), ())), preferred_element_type=jnp.float32
    )


def per_device(
    section_input, norm_gain, value_weight, attn_probs, out_weight, direction, curvature
):
    x_input = section_input[0]
    gain = norm_gain[0]
    w_val = value_weight[0]
    w_out = out_weight[0]
    w_dir = direction[0]
    probs = attn_probs[0]
    sections = lax.axis_size("section")
    place = lax.axis_index("section")
    tok_rows, width = x_input.shape
    heads = probs.shape[0]
    head_size = w_val.shape[0] // heads
    share_rows = tok_rows // lax.axis_size("tensor")
    share_start = lax.axis_index("tensor") * share_rows
    probs_wide = probs.astype(jnp.float32)

    def rows_of(array):
        return lax.dynamic_slice_in_dim(array, share_start, share_rows, 0)

    def mix(values):
        split = values.reshape(tok_rows, heads, head_size)
        return jnp.einsum("hqk,khd->qhd", probs, split, preferred_element_type=jnp.float32).reshape(
            tok_rows, heads * head_size
        )

    def unmix(grads):
        split = grads.reshape(tok_rows, heads, head_size)
        return jnp.einsum("hqk,qhd->khd", probs_wide, split).reshape(tok_rows, heads * head_size)

    xfull = x_input.astype(jnp.float32)
    rnorm = lax.rsqrt(jnp.mean(xfull * xfull, axis=-1, keepdims=True) + 1e-06)
    normed = (xfull * rnorm * gain).astype(jnp.bfloat16)
    values = contract_last(normed, w_val).astype(jnp.bfloat16)
    act = mix(values).astype(jnp.bfloat16)
    base = contract_last(act, w_dir)
    base_share = lax.psum_scatter(base, "tensor", scatter_dimension=0, tiled=True)
    xrows = rows_of(x_input).astype(jnp.float32)
    rrows = rows_of(rnorm)

    def tangent_terms(tnorm):
        tvals = contract_last(tnorm, w_val).astype(jnp.bfloat16)
        tmix = mix(tvals).astype(jnp.bfloat16)
        return contract_last(tmix, w_out)

    def adjoint_terms(adjoint):
        gmix = jnp.dot(adjoint, w_out, preferred_element_type=jnp.float32)
        gvals = unmix(gmix).astype(jnp.bfloat16)
        return jnp.dot(gvals, w_val, preferred_element_type=jnp.float32)

    def blank(array):
        return jnp.zeros((tok_rows, width), jnp.float32)

    mine = base_share.astype(jnp.bfloat16)
    for step in range(1, sections):
        pass_moved = from_behind(mine, "section", 1)
        tfloat = pass_moved.astype(jnp.float32)
        normed_rows = (
            gain
            * (rrows * tfloat - rrows**3 * xrows * jnp.mean(xrows * tfloat, axis=-1, keepdims=True))
        ).astype(jnp.bfloat16)
        tnorm = lax.all_gather(normed_rows, "tensor", axis=0, tiled=True)
        partial_sum = lax.cond(place == step, tangent_terms, blank, tnorm)
        share = lax.psum_scatter(partial_sum, "tensor", scatter_dimension=0, tiled=True)
        mine = (pass_moved.astype(jnp.float32) + (share + base_share)).astype(jnp.bfloat16)
    seed_rows = (rows_of(curvature).astype(jnp.float32) * mine.astype(jnp.float32)).astype(
        jnp.bfloat16
    )
    adjoint = lax.all_gather(seed_rows, "tensor", axis=0, tiled=True)
    for step in range(sections - 1):
        gpart = lax.cond(place == sections - 1 - step, adjoint_terms, blank, adjoint)
        gshare = lax.psum_scatter(
            gpart.astype(jnp.bfloat16), "tensor", scatter_dimension=0, tiled=True
        ).astype(jnp.float32)
        gxval = rrows * gain * gshare - rrows**3 * xrows * jnp.mean(
            xrows * gain * gshare, axis=-1, keepdims=True
        )
        passed = (rows_of(adjoint).astype(jnp.float32) + gxval).astype(jnp.bfloat16)
        moved = from_behind(passed, "section", -1)
        received = lax.all_gather(moved, "tensor", axis=0, tiled=True)
        adjoint = jnp.where(place == sections - 2 - step, received, adjoint)
    product = lax.psum_scatter(
        contract_first(adjoint, act).astype(jnp.bfloat16), "dp", scatter_dimension=0, tiled=True
    ).astype(jnp.float32)
    return product[None]


def solution(mesh):
    in_specs = (
        P("section", "dp", None),
        P("section", None),
        P("section", "tensor", None),
        P("section", "tensor", "dp", None),
        P("section", None, "tensor"),
        P("section", None, "tensor"),
        P("dp", None),
    )
    out_specs = P("section", "dp", "tensor")
    return jax.shard_map(
        per_device, mesh=mesh, in_specs=in_specs, out_specs=out_specs, check_vma=False
    )
```

profile of v0, /device:TPU:0, one launch (start us, length us, event | category | flops | bytes accessed | tf_op | source)
XLA Modules:
  0.0 239.2 jit_solution(9895617419510271331)
XLA Ops:
  6.5 1.5 fusion.2
  8.1 2.8 %convolution_convert_fusion.4 = bf16[128,384]{1,0:T(8,128)(2,1)S(1)} fusion(bf16[1,128,3072]{2,1,0:T(8,128)(2,1)} %param.11, f32[3072]{0:T(1024)} %bitcast.67, f32[128]{0:T(128)S(1)} %add_rsqrt_fusion, bf16[1,384,3072]{2,1,0:T(8,128)(2,1)} %param.13), kind=kOutput, calls=%fused_computation.11 | convolution fusion | flops 303611904 | bytes 3256832 | tf_op jit(solution)/shard_map/dot_general | solution.py:14
  10.9 0.1 copy.13
  11.0 0.2 convolution_convert_fusion.5
  11.2 2.0 fusion
  13.3 0.0 reduce-scatter.7.cloned.1.call-start
  13.4 38.3 %reduce-scatter.5.cloned.1.call-done = f32[32,3072]{1,0:T(8,128)} async-done(((f32[128,3072]{1,0:T(8,128)}), f32[32,3072]{1,0:T(8,128)}) %reduce-scatter.5.cloned.1.call-update) | async-done | bytes 393232 | tf_op jit(solution)/shard_map/reduce_scatter | solution.py:62
  51.6 1.7 convert_element_type.106
  53.3 3.4 %collective-permute-start = (bf16[32,3072]{1,0:T(8,128)(2,1)}, bf16[32,3072]{1,0:T(8,128)(2,1)S(1)}, u32[]{:S(2)}, u32[]{:S(2)}) collective-permute-start(bf16[32,3072]{1,0:T(8,128)(2,1)} %convert_element_type.106), channel_id=1, source_target_pairs={{0,4},{1,5},{2,6},{3,7},{8,12},{9,13},{10,14},{11,15},{16,20},{17,... | collective-permute-start | bytes 589832 | tf_op jit(solution)/shard_map/ppermute | solution.py:10
  56.7 0.8 fusion.22
  57.5 3.3 %collective-permute-done = bf16[32,3072]{1,0:T(8,128)(2,1)S(1)} collective-permute-done((bf16[32,3072]{1,0:T(8,128)(2,1)}, bf16[32,3072]{1,0:T(8,128)(2,1)S(1)}, u32[]{:S(2)}, u32[]{:S(2)}) %collective-permute-start) | collective-permute-done | bytes 196640 | tf_op jit(solution)/shard_map/ppermute | solution.py:10
  60.8 0.2 fusion.21
  61.0 0.2 fusion.15
  61.1 17.8 %all_gather.9 = bf16[128,3072]{1,0:T(8,128)(2,1)S(1)} all-gather(bf16[32,3072]{1,0:T(8,128)(2,1)S(1)} %fusion.15), channel_id=1, replica_groups=mesh['dp'=4,'section'=2,'tensor'=4] {'tensor'}, dimensions={0}, use_global_device_ids=true | all-gather | bytes 983040 | tf_op jit(solution)/shard_map/all_gather | solution.py:87
  78.9 1.3 conditional.2
  78.9 1.3 broadcast.49
  80.2 0.0 reduce-scatter.9.cloned.1.call-start
  80.3 42.2 %reduce-scatter.7.cloned.1.call-done = f32[32,3072]{1,0:T(8,128)} async-done(((f32[128,3072]{1,0:T(8,128)}), f32[32,3072]{1,0:T(8,128)}) %reduce-scatter.7.cloned.1.call-update) | async-done | bytes 393232 | tf_op jit(solution)/shard_map/reduce_scatter | solution.py:89
  122.5 1.2 multiply_convert_fusion
  123.7 17.9 %all_gather.10 = bf16[128,3072]{1,0:T(8,128)(2,1)S(1)} all-gather(bf16[32,3072]{1,0:T(8,128)(2,1)S(1)} %multiply_convert_fusion), channel_id=1, replica_groups=mesh['dp'=4,'section'=2,'tensor'=4] {'tensor'}, dimensions={0}, use_global_device_ids=true | all-gather | bytes 983040 | tf_op jit(solution)/shard_map/all_gather | solution.py:94
  141.6 1.0 conditional.3
  141.6 1.0 broadcast.50
  142.6 0.0 reduce-scatter.11.cloned.1.call-start
  142.7 26.2 %reduce-scatter.9.cloned.1.call-done = bf16[32,3072]{1,0:T(8,128)(2,1)} async-done(((bf16[128,3072]{1,0:T(8,128)(2,1)}), bf16[32,3072]{1,0:T(8,128)(2,1)}) %reduce-scatter.9.cloned.1.call-update) | async-done | bytes 196624 | tf_op jit(solution)/shard_map/reduce_scatter | solution.py:97
  168.8 1.2 fusion.19
  170.0 1.2 fusion.18
  171.3 1.3 collective-permute-start.1
  172.6 6.8 %collective-permute-done.1 = bf16[32,3072]{1,0:T(8,128)(2,1)} collective-permute-done((bf16[32,3072]{1,0:T(8,128)(2,1)S(1)}, bf16[32,3072]{1,0:T(8,128)(2,1)}, u32[]{:S(2)}, u32[]{:S(2)}) %collective-permute-start.1) | collective-permute-done | bytes 196640 | tf_op jit(solution)/shard_map/ppermute | solution.py:10
  179.4 17.9 %all_gather.11 = bf16[128,3072]{1,0:T(8,128)(2,1)S(1)} all-gather(bf16[32,3072]{1,0:T(8,128)(2,1)} %collective-permute-done.1), channel_id=1, replica_groups=mesh['dp'=4,'section'=2,'tensor'=4] {'tensor'}, dimensions={0}, use_global_device_ids=true | all-gather | bytes 983040 | tf_op jit(solution)/shard_map/all_gather | solution.py:105
  197.3 2.2 convolution_convert_fusion.3
  199.5 31.0 %reduce-scatter.11.cloned.1.call-done = bf16[768,384]{1,0:T(8,128)(2,1)} async-done(((bf16[3072,384]{1,0:T(8,128)(2,1)}), bf16[768,384]{1,0:T(8,128)(2,1)}) %reduce-scatter.11.cloned.1.call-update) | async-done | bytes 589840 | tf_op jit(solution)/shard_map/reduce_scatter | solution.py:107
  230.5 2.2 bitcast_convert_fusion
  (20 shorter events, 0.1 us)
Async XLA Ops:
  6.5 4.7 %copy-start = (bf16[1,3072,384]{2,1,0:T(8,128)(2,1)S(1)}, bf16[1,3072,384]{2,1,0:T(8,128)(2,1)}, u32[]{:S(2)}) copy-start(bf16[1,3072,384]{2,1,0:T(8,128)(2,1)} %param.16) | copy-start | bytes 7077892
  6.5 4.5 %copy-start.3 = (bf16[1,3,128,128]{3,2,1,0:T(8,128)(2,1)S(1)}, bf16[1,3,128,128]{3,2,1,0:T(8,128)(2,1)}, u32[]{:S(2)}) copy-start(bf16[1,3,128,128]{3,2,1,0:T(8,128)(2,1)} %param.14) | copy-start | bytes 294916
  6.5 45.1 %reduce-scatter.5.cloned.1.call-start = ((), (), s32[]{:S(2)}) async-start(), calls=%async_computation.4 | async-start | bytes 1966080 | tf_op jit(solution)/shard_map/reduce_scatter | solution.py:62
  8.1 3.1 %copy-start.6 = (f32[128]{0:T(128)}, f32[128]{0:T(128)S(1)}, u32[]{:S(2)}) copy-start(f32[128]{0:T(128)S(1)} %add_rsqrt_fusion) | copy-start | bytes 1540
  11.2 49.6 %copy-start.2 = (bf16[1,128,3072]{2,1,0:T(8,128)(2,1)S(1)}, bf16[1,128,3072]{2,1,0:T(8,128)(2,1)}, u32[]{:S(2)}) copy-start(bf16[1,128,3072]{2,1,0:T(8,128)(2,1)} %param.11) | copy-start | bytes 2359300
  11.2 49.7 %copy-start.4 = (f32[1,3072]{1,0:T(1,128)S(1)}, f32[1,3072]{1,0:T(1,128)}, u32[]{:S(2)}) copy-start(f32[1,3072]{1,0:T(1,128)} %param.12) | copy-start | bytes 36868
  13.3 109.2 %reduce-scatter.7.cloned.1.call-start = ((), (), s32[]{:S(2)}) async-start(), calls=%async_computation.5 | async-start | bytes 1966080 | tf_op jit(solution)/shard_map/reduce_scatter | solution.py:89
  53.3 7.4 %collective-permute-start = (bf16[32,3072]{1,0:T(8,128)(2,1)}, bf16[32,3072]{1,0:T(8,128)(2,1)S(1)}, u32[]{:S(2)}, u32[]{:S(2)}) collective-permute-start(bf16[32,3072]{1,0:T(8,128)(2,1)} %convert_element_type.106), channel_id=1, source_target_pairs={{0,4},{1,5},{2,6},{3,7},{8,12},{9,13},{10,14},{11,15},{16,20},{17,... | collective-permute-start | bytes 589832 | tf_op jit(solution)/shard_map/ppermute | solution.py:10
  57.5 21.4 %copy-start.5 = (f32[32]{0:T(128)}, f32[32]{0:T(128)S(1)}, u32[]{:S(2)}) copy-start(f32[32]{0:T(128)S(1)} %get-tuple-element.37) | copy-start | bytes 388
  80.2 88.6 %reduce-scatter.9.cloned.1.call-start = ((), (), s32[]{:S(2)}) async-start(), calls=%async_computation.6 | async-start | bytes 983040 | tf_op jit(solution)/shard_map/reduce_scatter | solution.py:97
  142.6 87.9 %reduce-scatter.11.cloned.1.call-start = ((), (), s32[]{:S(2)}) async-start(), calls=%async_computation.7 | async-start | bytes 2949120 | tf_op jit(solution)/shard_map/reduce_scatter | solution.py:107
  171.3 8.1 %collective-permute-start.1 = (bf16[32,3072]{1,0:T(8,128)(2,1)S(1)}, bf16[32,3072]{1,0:T(8,128)(2,1)}, u32[]{:S(2)}, u32[]{:S(2)}) collective-permute-start(bf16[32,3072]{1,0:T(8,128)(2,1)S(1)} %fusion.18), channel_id=1, source_target_pairs={{4,0},{5,1},{6,2},{7,3},{12,8},{13,9},{14,10},{15,11},{20,16},{21,... | collective-permute-start | bytes 589832 | tf_op jit(solution)/shard_map/ppermute | solution.py:10
Sparse Core Ops, SparseCore 0:
  13.4 38.1 reduce-scatter.4
  80.4 42.0 reduce-scatter.6
  142.7 26.0 reduce-scatter.8
  199.7 30.7 reduce-scatter.10
where the time goes:
time: 240 us; the launch traced here: 239 us
  waiting for transfers between devices  148 us (62%)
  blocking collectives  53.6 us (22%)
  between operations  13.2 us (6%)
  other arithmetic  10.1 us (4%)
  matrix products  7.23 us (3%)
  starting transfers between devices  4.8 us (2%)
  local copies, waits for them, and re-layouts  2.44 us (1%)
    reduce_scatter x1, waiting for transfers between devices, per_device(): lax.psum_scatter(partial_sum, 'tensor', scatter_dimension=0, tiled=True)  42.2 us
    reduce_scatter x1, waiting for transfers between devices, per_device(): lax.psum_scatter(base, 'tensor', scatter_dimension=0, tiled=True)  38.3 us
    reduce_scatter x1, waiting for transfers between devices, per_device(): lax.psum_scatter(contract_first(adjoint, act).astype(jnp.bfloat16), 'dp',...  31 us
    reduce_scatter x1, waiting for transfers between devices, per_device(): lax.psum_scatter(gpart.astype(jnp.bfloat16), 'tensor', scatter_dimension=...  26.2 us
    all_gather x1, blocking collectives, per_device(): received = lax.all_gather(moved, 'tensor', axis=0, tiled=True)  17.9 us
    all_gather x1, blocking collectives, per_device(): adjoint = lax.all_gather(seed_rows, 'tensor', axis=0, tiled=True)  17.9 us
    all_gather x1, blocking collectives, per_device(): tnorm = lax.all_gather(normed_rows, 'tensor', axis=0, tiled=True)  17.8 us
    ppermute x2, waiting for transfers between devices, from_behind(): return lax.ppermute(block, axis, route)  10.1 us
  transfers between devices with their start and end apart: 6, of which 6 were waited for; matrix products, arithmetic and copies ran while one was open for 0% of the time, Pallas kernels for 0%

commit v1 on v0

v1 whole, which is shorter than its diff:
```python
import functools

import jax
import jax.numpy as jnp
from jax import lax
from jax.experimental import pallas as pl
from jax.experimental.pallas import tpu as pltpu
from jax.sharding import PartitionSpec as P

MESH = pl.DeviceIdType.MESH
BF = jnp.bfloat16
F32 = jnp.float32


def dot_nt(a, b):
    return lax.dot_general(a, b, (((1,), (1,)), ((), ())), preferred_element_type=F32)


def dot_tn(a, b):
    return lax.dot_general(a, b, (((0,), (0,)), ((), ())), preferred_element_type=F32)


def dot_nn(a, b):
    return lax.dot_general(a, b, (((1,), (0,)), ((), ())), preferred_element_type=F32)


def kernel(
    fused, S, T, N,
    x_ref, gain_ref, probs_ref, wv_hbm, wd_hbm, wo_hbm, curv_hbm,
    *rest,
):
    if fused:
        prod_ref, rest = rest[0], rest[1:]
    else:
        gout_ref, actout_ref, rest = rest[0], rest[1], rest[2:]
    (
        wv, wd, wo, curv, act, part, partb, in_a, in_d, in_f, gpartb, normed, tn, gfull, trow, grow,
        actall, gall,
        load_sem, act_send, act_recv, a_send, a_recv, tn_send, tn_recv, d_send, d_recv,
        s_send, s_recv, f_send, f_recv, h_send, h_recv, x_send, x_recv,
    ) = rest
    d = lax.axis_index("dp")
    s = lax.axis_index("section")
    i = lax.axis_index("tensor")
    tok, width = x_ref.shape
    rows = tok // T
    heads = probs_ref.shape[0]
    hd = wv.shape[0] // heads
    feats = width // N
    CH = 512 if width % 512 == 0 else width
    chunks = [slice(c, c + CH) for c in range(0, width, CH)]

    def rows_at(j):
        return pl.ds(pl.multiple_of(j * rows, rows), rows)

    def feats_at(j):
        return pl.ds(pl.multiple_of(j * feats, 128), feats)

    def peer(me, k, n):
        return lax.rem(me + k, n)

    loads = [
        pltpu.make_async_copy(src, dst, load_sem.at[k])
        for k, (src, dst) in enumerate(((wv_hbm, wv), (wd_hbm, wd), (wo_hbm, wo), (curv_hbm, curv)))
    ]
    for copy in loads:
        copy.start()

    barrier = pltpu.get_barrier_semaphore()

    def greet(dev):
        pl.semaphore_signal(barrier, inc=1, device_id=dev, device_id_type=MESH)

    for k in range(1, T):
        greet({"dp": d, "section": s, "tensor": peer(i, k, T)})
    for k in range(1, N):
        greet({"dp": peer(d, k, N), "section": s, "tensor": i})
    for low in range(S - 1):
        wide = N if (fused and low == 0) else 1

        @pl.when(s == low)
        def _():
            for k in range(wide):
                for j in range(T):
                    greet({"dp": peer(d, k, N), "section": s + 1, "tensor": j})

        @pl.when(s == low + 1)
        def _():
            for k in range(wide):
                for j in range(T):
                    greet({"dp": peer(d, k, N), "section": s - 1, "tensor": j})

    gain = gain_ref[...]
    xf = x_ref[...].astype(F32)
    rnorm = lax.rsqrt(jnp.mean(xf * xf, axis=-1, keepdims=True) + 1e-06)
    normed[...] = (xf * rnorm * gain).astype(BF)

    def mix(vals):
        return jnp.concatenate(
            [dot_nn(probs_ref[h], vals[:, h * hd : (h + 1) * hd]) for h in range(heads)], axis=1
        )

    loads[0].wait()
    act[...] = mix(dot_nt(normed[...], wv[...]).astype(BF)).astype(BF)

    for here in range(S):
        count = T - 1 + N - 1
        for low in (here - 1, here):
            if 0 <= low < S - 1:
                count += T * (N if (fused and low == 0) else 1)

        @pl.when(s == here)
        def _():
            pl.semaphore_wait(barrier, count)

    def remote(src, dst, send, recv, dev):
        return pltpu.make_async_remote_copy(
            src_ref=src, dst_ref=dst, send_sem=send, recv_sem=recv,
            device_id=dev, device_id_type=MESH,
        )

    def at(dd, ss, jj):
        return {"dp": dd, "section": ss, "tensor": jj}

    def copy_act(k, owner):
        return remote(act, actall.at[owner], act_send.at[k], act_recv.at[k], at(peer(d, k, N), s, i))

    def copy_a(j, owner):
        return remote(partb.at[rows_at(j)], in_a.at[owner], a_send.at[j], a_recv.at[owner], at(d, s + 1, j))

    def copy_tn(k, owner):
        return remote(
            tn.at[rows_at(owner)], tn.at[rows_at(owner)], tn_send.at[k], tn_recv.at[k], at(d, s, peer(i, k, T))
        )

    def copy_d(k):
        j = peer(i, k, T)
        return remote(partb.at[rows_at(j)], in_d.at[k - 1], d_send.at[k], d_recv.at[k], at(d, s, j))

    def copy_s(k, owner):
        return remote(
            gfull.at[rows_at(owner)], gfull.at[rows_at(owner)], s_send.at[k], s_recv.at[k],
            at(d, s, peer(i, k, T)),
        )

    def copy_f(k):
        j = peer(i, k, T)
        return remote(gpartb.at[rows_at(j)], in_f.at[k - 1], f_send.at[k], f_recv.at[k], at(d, s, j))

    def copy_h(j, owner):
        return remote(grow, gfull.at[rows_at(owner)], h_send.at[0, j], h_recv.at[0, owner], at(d, s - 1, j))

    def copy_hd(k, j, owner):
        dd = peer(d, k, N)
        return remote(
            grow.at[:, feats_at(dd)], gall.at[lax.rem(d, N), rows_at(owner)],
            h_send.at[k, j], h_recv.at[k, owner], at(dd, s - 1, j),
        )

    def land_hd(k, owner):
        src = peer(d, N - k, N)
        return remote(
            grow.at[:, feats_at(d)], gall.at[src, rows_at(owner)],
            h_send.at[k, owner], h_recv.at[k, owner], at(d, s, i),
        )

    def copy_x(k):
        dd = peer(d, k, N)
        return remote(gfull.at[:, feats_at(dd)], gall.at[d], x_send.at[k], x_recv.at[k], at(dd, s, i))

    def land_x(k):
        src = peer(d, N - k, N)
        return remote(gfull.at[:, feats_at(d)], gall.at[src], x_send.at[k], x_recv.at[k], at(d, s, i))

    if fused:
        for k in range(1, N):
            copy_act(k, d).start()
        actall[d] = act[...]

    xrows = x_ref[rows_at(i)].astype(F32)
    rrows = lax.rsqrt(jnp.mean(xrows * xrows, axis=-1, keepdims=True) + 1e-06)

    loads[1].wait()
    for c in chunks:
        base = dot_nt(act[...], wd[c, :])
        part[:, c] = base

    loads[2].wait()
    loads[3].wait()

    @pl.when(s == 0)
    def _():
        partb[...] = part[...].astype(BF)

    @pl.when(s > 0)
    def _():
        total = None
        for j in range(T):
            remote(partb.at[rows_at(j)], in_a.at[j], a_send.at[j], a_recv.at[j], at(d, s, i)).wait_recv()
        for j in range(T):
            piece = in_a[j].astype(F32)
            total = piece if total is None else total + piece
        tfloat = total.astype(BF).astype(F32)
        trow[...] = tfloat
        tn[rows_at(i)] = (
            gain * (rrows * tfloat - rrows**3 * xrows * jnp.mean(xrows * tfloat, axis=-1, keepdims=True))
        ).astype(BF)
        for k in range(1, T):
            copy_tn(k, i).start()
        for k in range(1, T):
            copy_tn(k, peer(i, T - k, T)).wait_recv()
        tmix = mix(dot_nt(tn[...], wv[...]).astype(BF)).astype(BF)
        for c in chunks:
            part[:, c] = part[:, c] + dot_nt(tmix, wo[c, :])
        part[rows_at(i)] = part[rows_at(i)] + trow[...]
        partb[...] = part[...].astype(BF)
        for k in range(1, T):
            copy_tn(k, i).wait_send()

    if S > 1:

        @pl.when(s < S - 1)
        def _():
            for j in range(T):
                copy_a(j, i).start()

    @pl.when(s == S - 1)
    def _():
        for k in range(1, T):
            copy_d(k).start()
        total = part[rows_at(i)]
        for k in range(1, T):
            copy_d(k).wait_recv()
        for k in range(1, T):
            total = total + in_d[k - 1].astype(F32)
        tlast = total.astype(BF).astype(F32)
        gfull[rows_at(i)] = (curv[rows_at(i)].astype(F32) * tlast).astype(BF)
        for k in range(1, T):
            copy_s(k, i).start()
        for k in range(1, T):
            copy_s(k, peer(i, T - k, T)).wait_recv()
        for k in range(1, T):
            copy_s(k, i).wait_send()
            copy_d(k).wait_send()

    if S > 1:

        @pl.when(s < S - 1)
        def _():
            for j in range(T):
                copy_a(j, i).wait_send()

        def gather_rows():
            for j in range(T):
                remote(grow, gfull.at[rows_at(j)], h_send.at[0, j], h_recv.at[0, j], at(d, s, i)).wait_recv()

        if fused:
            if S > 2:

                @pl.when(jnp.logical_and(s > 0, s < S - 1))
                def _():
                    gather_rows()

            @pl.when(s == 0)
            def _():
                for k in range(N):
                    for j in range(T):
                        land_hd(k, j).wait_recv()
        else:

            @pl.when(s < S - 1)
            def _():
                gather_rows()

        @pl.when(s > 0)
        def _():
            gm = dot_nn(gfull[...], wo[...]).astype(BF)
            gv = jnp.concatenate(
                [dot_tn(probs_ref[h], gm[:, h * hd : (h + 1) * hd]) for h in range(heads)], axis=1
            ).astype(BF)
            for c in chunks:
                gc = dot_nn(gv, wv[:, c])
                part[:, c] = gc
                gpartb[:, c] = gc.astype(BF)
            for k in range(1, T):
                copy_f(k).start()
            total = part[rows_at(i)]
            for k in range(1, T):
                copy_f(k).wait_recv()
            for k in range(1, T):
                total = total + in_f[k - 1].astype(F32)
            scaled = gain * total
            gx = rrows * scaled - rrows**3 * xrows * jnp.mean(xrows * scaled, axis=-1, keepdims=True)
            grow[...] = (gfull[rows_at(i)].astype(F32) + gx).astype(BF)

            def plain():
                for j in range(T):
                    copy_h(j, i).start()
                for j in range(T):
                    copy_h(j, i).wait_send()

            if fused:

                @pl.when(s == 1)
                def _():
                    for k in range(N):
                        for j in range(T):
                            copy_hd(k, j, i).start()
                    for k in range(N):
                        for j in range(T):
                            copy_hd(k, j, i).wait_send()

                if S > 2:
                    pl.when(s > 1)(plain)
            else:
                plain()
            for k in range(1, T):
                copy_f(k).wait_send()

    if fused:

        def spread():
            for k in range(1, N):
                copy_x(k).start()
            gall[d] = gfull[:, feats_at(d)]
            for k in range(1, N):
                land_x(k).wait_recv()
            for k in range(1, N):
                copy_x(k).wait_send()

        if S > 1:
            pl.when(s > 0)(spread)
        else:
            spread()
        for k in range(1, N):
            copy_act(k, peer(d, N - k, N)).wait_recv()
        prod_ref[...] = dot_tn(
            gall[...].reshape(N * tok, feats), actall[...].reshape(N * tok, act.shape[1])
        )
        for k in range(1, N):
            copy_act(k, d).wait_send()
    else:
        gout_ref[...] = gfull[...]
        actout_ref[...] = act[...]


def per_device(section_input, norm_gain, value_weight, attn_probs, out_weight, direction, curvature):
    x = section_input[0]
    w_val = value_weight[0]
    w_out = out_weight[0]
    w_dir = direction[0]
    probs = attn_probs[0]
    S = lax.axis_size("section")
    T = lax.axis_size("tensor")
    N = lax.axis_size("dp")
    tok, width = x.shape
    hf = w_val.shape[0]
    rows = tok // T
    feats = width // N
    fused = feats % 128 == 0 and feats * N == width
    vm = functools.partial(pl.BlockSpec, memory_space=pltpu.VMEM)
    hbm = functools.partial(pl.BlockSpec, memory_space=pl.ANY)
    if fused:
        outs = jax.ShapeDtypeStruct((feats, hf), F32)
        out_specs = vm()
    else:
        outs = (jax.ShapeDtypeStruct((tok, width), BF), jax.ShapeDtypeStruct((tok, hf), BF))
        out_specs = (vm(), vm())
    sem = pltpu.SemaphoreType.DMA
    wide = N if fused else 1
    scratch = [
        pltpu.VMEM((hf, width), BF),
        pltpu.VMEM((width, hf), BF),
        pltpu.VMEM((width, hf), BF),
        pltpu.VMEM((tok, width), BF),
        pltpu.VMEM((tok, hf), BF),
        pltpu.VMEM((tok, width), F32),
        pltpu.VMEM((tok, width), BF),
        pltpu.VMEM((T, rows, width), BF),
        pltpu.VMEM((T, rows, width), BF),
        pltpu.VMEM((T, rows, width), BF),
        pltpu.VMEM((tok, width), BF),
        pltpu.VMEM((tok, width), BF),
        pltpu.VMEM((tok, width), BF),
        pltpu.VMEM((tok, width), BF),
        pltpu.VMEM((rows, width), F32),
        pltpu.VMEM((rows, width), BF),
        pltpu.VMEM((wide, tok, hf), BF),
        pltpu.VMEM((wide, tok, feats if fused else 128), BF),
        sem((4,)),
        sem((N,)), sem((N,)),
        sem((T,)), sem((T,)),
        sem((T,)), sem((T,)),
        sem((T,)), sem((T,)),
        sem((T,)), sem((T,)),
        sem((T,)), sem((T,)),
        sem((wide, T)), sem((wide, T)),
        sem((N,)), sem((N,)),
    ]
    result = pl.pallas_call(
        functools.partial(kernel, fused, S, T, N),
        out_shape=outs,
        in_specs=[vm(), vm(), vm(), hbm(), hbm(), hbm(), hbm()],
        out_specs=out_specs,
        scratch_shapes=scratch,
        compiler_params=pltpu.CompilerParams(
            collective_id=0, has_side_effects=True, vmem_limit_bytes=56 * 1024 * 1024
        ),
    )(x, norm_gain, probs, w_val, w_dir, w_out, curvature)
    if fused:
        return result[None]
    adjoint, act = result
    product = lax.psum_scatter(
        dot_tn(adjoint, act).astype(BF), "dp", scatter_dimension=0, tiled=True
    ).astype(F32)
    return product[None]


def solution(mesh):
    in_specs = (
        P("section", "dp", None),
        P("section", None),
        P("section", "tensor", None),
        P("section", "tensor", "dp", None),
        P("section", None, "tensor"),
        P("section", None, "tensor"),
        P("dp", None),
    )
    out_specs = P("section", "dp", "tensor")
    return jax.shard_map(
        per_device, mesh=mesh, in_specs=in_specs, out_specs=out_specs, check_vma=False
    )
```

time: 240 us -> 129 us (0.54)
  the two profiles are of different devices: /device:TPU:0 before, /device:TPU:23 now
where the time goes in v1:
time: 129 us
  Pallas kernels  127 us (98%)
  local copies, waits for them, and re-layouts  2.36 us (2%)
    pallas_call x1, Pallas kernels, per_device(): pl.pallas_call(functools.partial(kernel, fused, S, T, N), out_shape=outs,...  127 us

profile of v1, /device:TPU:23, one launch (start us, length us, event | category | flops | bytes accessed | tf_op | source)
XLA Modules:
  0.0 129.2 jit_solution(2873006483487212699)
XLA Ops:
  0.0 126.8 %shard_map.73 = f32[768,384]{1,0:T(8,128)} custom-call(bf16[128,3072]{1,0:T(8,128)(2,1)} %bitcast.10, f32[1,3072]{1,0:T(1,128)} %gain_ref.1, bf16[3,128,128]{2,1,0:T(8,128)(2,1)} %bitcast.11, bf16[384,3072]{1,0:T(8,128)(2,1)} %bitcast.7, bf16[3072,384]{1,0:T(8,128)(2,1)} %bitcast.8, bf16[3072,384]{1,0:T(8,128)(2,1)} %bitcast.9, bf16[128,3072]{1,0:T(8,128)(2,1)} %curv_hbm.1), custom_call_target="tpu_custom_call" | custom-call | tf_op jit(solution)/shard_map/pallas_call | solution.py:400
  126.8 2.4 %copy.9 = f32[1,768,384]{2,1,0:T(8,128)} copy(f32[1,768,384]{2,1,0:T(8,128)} %bitcast.6) | data formatting | bytes 2359296

commit v2 on v1

--- a/solution.py
+++ b/solution.py
@@ -344,6 +344,309 @@
         actout_ref[...] = act[...]
 
 
+def kernel_pair(
+    T, N,
+    x_ref, gain_ref, probs_ref, wv_hbm, wd_hbm, wo_hbm, curv_hbm,
+    prod_ref,
+    wv, wd, wo, curv, act, part, partb, in_a, in_d, in_f, gpartb, normed, tn, gfull, trow, xrow, grow,
+    gain1, actall, gall,
+    load_sem, act_send, act_recv, g_send, g_recv, a_send, a_recv, c_send, c_recv, d_send, d_recv,
+    e_send, e_recv, f_send, f_recv, h_send, h_recv, x_send, x_recv,
+):
+    d = lax.axis_index("dp")
+    s = lax.axis_index("section")
+    i = lax.axis_index("tensor")
+    tok, width = x_ref.shape
+    rows = tok // T
+    half = rows // 2
+    heads = probs_ref.shape[0]
+    hd = wv.shape[0] // heads
+    feats = width // N
+    CH = 512 if width % 512 == 0 else width
+    chunks = [slice(c, c + CH) for c in range(0, width, CH)]
+
+    def own(ss, jj):
+        return pl.ds(pl.multiple_of(jj * rows + (1 - ss) * half, half), half)
+
+    def feats_at(j):
+        return pl.ds(pl.multiple_of(j * feats, 128), feats)
+
+    def peer(me, k, n):
+        return lax.rem(me + k, n)
+
+    def at(dd, ss, jj):
+        return {"dp": dd, "section": ss, "tensor": jj}
+
+    def remote(src, dst, send, recv, dev):
+        return pltpu.make_async_remote_copy(
+            src_ref=src, dst_ref=dst, send_sem=send, recv_sem=recv,
+            device_id=dev, device_id_type=MESH,
+        )
+
+    loads = [
+        pltpu.make_async_copy(src, dst, load_sem.at[k])
+        for k, (src, dst) in enumerate(((wv_hbm, wv), (wd_hbm, wd), (wo_hbm, wo), (curv_hbm, curv)))
+    ]
+    for copy in loads:
+        copy.start()
+
+    barrier = pltpu.get_barrier_semaphore()
+    for a in range(N):
+        for b in range(2):
+            for c in range(T):
+                if a or b or c:
+                    pl.semaphore_signal(
+                        barrier, inc=1, device_id=at(peer(d, a, N), peer(s, b, 2), peer(i, c, T)),
+                        device_id_type=MESH,
+                    )
+
+    def mix(vals):
+        return jnp.concatenate(
+            [dot_nn(probs_ref[h], vals[:, h * hd : (h + 1) * hd]) for h in range(heads)], axis=1
+        )
+
+    gain = gain_ref[...]
+    xf = x_ref[...].astype(F32)
+    rnorm = lax.rsqrt(jnp.mean(xf * xf, axis=-1, keepdims=True) + 1e-06)
+    normed[...] = (xf * rnorm * gain).astype(BF)
+    loads[0].wait()
+    act[...] = mix(dot_nt(normed[...], wv[...]).astype(BF)).astype(BF)
+    pl.semaphore_wait(barrier, N * 2 * T - 1)
+
+    def copy_act(k, owner):
+        return remote(act, actall.at[owner], act_send.at[k], act_recv.at[k], at(peer(d, k, N), s, i))
+
+    lend = (
+        remote(x_ref.at[own(0, i)], xrow, g_send.at[0], g_recv.at[0], at(d, 0, i)),
+        remote(gain_ref, gain1, g_send.at[1], g_recv.at[1], at(d, 0, i)),
+    )
+
+    loads[1].wait()
+
+    def exchange(source, landing, send, recv, home, run):
+        for ss in (1 - home, home):
+            for k in range(T):
+                if ss == home and k == 0:
+                    continue
+                j = peer(i, k, T)
+                run(remote(source.at[own(ss, j)], landing.at[k], send.at[ss, k], recv.at[k], at(d, ss, j)))
+
+    def collect(source, landing, send, recv, home, local):
+        first = 1 if local is not None else 0
+        for k in range(first, T):
+            remote(source.at[own(s, i)], landing.at[k], send.at[0, k], recv.at[k], at(d, s, i)).wait_recv()
+        total = local
+        for k in range(first, T):
+            piece = landing[k].astype(F32)
+            total = piece if total is None else total + piece
+        return total
+
+    def spread_rows(buf, send, recv, me, run):
+        for k in range(T):
+            if me == 1 and k == 0:
+                continue
+            run(remote(buf.at[own(me, i)], buf.at[own(me, i)], send.at[k], recv.at[me, k], at(d, 1, peer(i, k, T))))
+
+    def gather_rows(buf, send, recv):
+        for ss in (1, 0):
+            for k in range(T):
+                if ss == 1 and k == 0:
+                    continue
+                src = own(ss, peer(i, T - k, T))
+                remote(buf.at[src], buf.at[src], send.at[k], recv.at[ss, k], at(d, s, i)).wait_recv()
+
+    def start(copy):
+        copy.start()
+
+    def ended(copy):
+        copy.wait_send()
+
+    def tangent_rows(total, xr, gn):
+        tb = total.astype(BF).astype(F32)
+        rr = lax.rsqrt(jnp.mean(xr * xr, axis=-1, keepdims=True) + 1e-06)
+        trow[...] = tb
+        tn[own(s, i)] = (
+            gn * (rr * tb - rr**3 * xr * jnp.mean(xr * tb, axis=-1, keepdims=True))
+        ).astype(BF)
+
+    def seed_rows(total):
+        tb = (total + trow[...]).astype(BF).astype(F32)
+        gfull[own(s, i)] = (curv[own(s, i)].astype(F32) * tb).astype(BF)
+
+    def adjoint_rows(total, xr, gn):
+        rr = lax.rsqrt(jnp.mean(xr * xr, axis=-1, keepdims=True) + 1e-06)
+        scaled = gn * total
+        gx = rr * scaled - rr**3 * xr * jnp.mean(xr * scaled, axis=-1, keepdims=True)
+        grow[...] = (gfull[own(s, i)].astype(F32) + gx).astype(BF)
+
+    def hand_over(me, run):
+        for k in range(N):
+            for j in range(T):
+                if me == 0 and k == 0 and j == 0:
+                    continue
+                dd = peer(d, k, N)
+                run(remote(
+                    grow.at[:, feats_at(dd)], gall.at[d, own(me, i)],
+                    h_send.at[k, j], h_recv.at[me, k, j], at(dd, 0, peer(i, j, T)),
+                ))
+
+    @pl.when(s == 0)
+    def _():
+        for c in chunks:
+            base = dot_nt(act[...], wd[c, :])
+            part[:, c] = base
+            partb[:, c] = base.astype(BF)
+        exchange(partb, in_a, a_send, a_recv, 0, start)
+        for k in range(1, N):
+            copy_act(k, d).start()
+        actall[d] = act[...]
+        for copy in lend:
+            copy.wait_recv()
+        xr = xrow[...].astype(F32)
+        gn = gain1[...]
+        tangent_rows(collect(partb, in_a, a_send, a_recv, 0, part[own(0, i)]), xr, gn)
+        spread_rows(tn, c_send, c_recv, 0, start)
+        loads[2].wait()
+        loads[3].wait()
+        seed_rows(collect(partb, in_d, d_send, d_recv, 1, None))
+        spread_rows(gfull, e_send, e_recv, 0, start)
+        adjoint_rows(collect(gpartb, in_f, f_send, f_recv, 1, None), xr, gn)
+        hand_over(0, start)
+        gall[d, own(0, i)] = grow[:, feats_at(d)]
+        for k in range(1, N):
+            copy_act(k, peer(d, N - k, N)).wait_recv()
+        for ss in (0, 1):
+            for k in range(N):
+                for j in range(T):
+                    if ss == 0 and k == 0 and j == 0:
+                        continue
+                    remote(
+                        grow.at[:, feats_at(d)],
+                        gall.at[peer(d, N - k, N), own(ss, peer(i, T - j, T))],
+                        h_send.at[k, j], h_recv.at[ss, k, j], at(d, s, i),
+                    ).wait_recv()
+        exchange(partb, in_a, a_send, a_recv, 0, ended)
+        spread_rows(tn, c_send, c_recv, 0, ended)
+        spread_rows(gfull, e_send, e_recv, 0, ended)
+        hand_over(0, ended)
+
+    @pl.when(s == 1)
+    def _():
+        for copy in lend:
+            copy.start()
+        for k in range(1, N):
+            copy_act(k, d).start()
+        actall[d] = act[...]
+        for c in chunks:
+            part[:, c] = dot_nt(act[...], wd[c, :])
+        loads[2].wait()
+        loads[3].wait()
+        xr = x_ref[own(1, i)].astype(F32)
+        tangent_rows(collect(partb, in_a, a_send, a_recv, 0, None), xr, gain)
+        spread_rows(tn, c_send, c_recv, 1, start)
+        gather_rows(tn, c_send, c_recv)
+        tmix = mix(dot_nt(tn[...], wv[...]).astype(BF)).astype(BF)
+        for c in chunks:
+            more = part[:, c] + dot_nt(tmix, wo[c, :])
+            part[:, c] = more
+            partb[:, c] = more.astype(BF)
+        exchange(partb, in_d, d_send, d_recv, 1, start)
+        seed_rows(collect(partb, in_d, d_send, d_recv, 1, part[own(1, i)]))
+        spread_rows(gfull, e_send, e_recv, 1, start)
+        gather_rows(gfull, e_send, e_recv)
+        gm = dot_nn(gfull[...], wo[...]).astype(BF)
+        gv = jnp.concatenate(
+            [dot_tn(probs_ref[h], gm[:, h * hd : (h + 1) * hd]) for h in range(heads)], axis=1
+        ).astype(BF)
+        for c in chunks:
+            gc = dot_nn(gv, wv[:, c])
+            part[:, c] = gc
+            gpartb[:, c] = gc.astype(BF)
+        exchange(gpartb, in_f, f_send, f_recv, 1, start)
+
+        def copy_x(k):
+            dd = peer(d, k, N)
+            return remote(gfull.at[:, feats_at(dd)], gall.at[d], x_send.at[k], x_recv.at[k], at(dd, s, i))
+
+        for k in range(1, N):
+            copy_x(k).start()
+        adjoint_rows(collect(gpartb, in_f, f_send, f_recv, 1, part[own(1, i)]), xr, gain)
+        hand_over(1, start)
+        gall[d] = gfull[:, feats_at(d)]
+        for k in range(1, N):
+            copy_act(k, peer(d, N - k, N)).wait_recv()
+        for k in range(1, N):
+            src = peer(d, N - k, N)
+            remote(gfull.at[:, feats_at(d)], gall.at[src], x_send.at[k], x_recv.at[k], at(d, s, i)).wait_recv()
+        for copy in lend:
+            copy.wait_send()
+        for k in range(1, N):
+            copy_x(k).wait_send()
+        spread_rows(tn, c_send, c_recv, 1, ended)
+        exchange(partb, in_d, d_send, d_recv, 1, ended)
+        spread_rows(gfull, e_send, e_recv, 1, ended)
+        exchange(gpartb, in_f, f_send, f_recv, 1, ended)
+        hand_over(1, ended)
+
+    prod_ref[...] = dot_tn(
+        gall[...].reshape(N * tok, feats), actall[...].reshape(N * tok, act.shape[1])
+    )
+    for k in range(1, N):
+        copy_act(k, d).wait_send()
+
+
+def call_pair(T, N, x, norm_gain, probs, w_val, w_dir, w_out, curvature):
+    tok, width = x.shape
+    hf = w_val.shape[0]
+    half = tok // T // 2
+    feats = width // N
+    vm = functools.partial(pl.BlockSpec, memory_space=pltpu.VMEM)
+    hbm = functools.partial(pl.BlockSpec, memory_space=pl.ANY)
+    sem = pltpu.SemaphoreType.DMA
+    scratch = [
+        pltpu.VMEM((hf, width), BF),
+        pltpu.VMEM((width, hf), BF),
+        pltpu.VMEM((width, hf), BF),
+        pltpu.VMEM((tok, width), BF),
+        pltpu.VMEM((tok, hf), BF),
+        pltpu.VMEM((tok, width), F32),
+        pltpu.VMEM((tok, width), BF),
+        pltpu.VMEM((T, half, width), BF),
+        pltpu.VMEM((T, half, width), BF),
+        pltpu.VMEM((T, half, width), BF),
+        pltpu.VMEM((tok, width), BF),
+        pltpu.VMEM((tok, width), BF),
+        pltpu.VMEM((tok, width), BF),
+        pltpu.VMEM((tok, width), BF),
+        pltpu.VMEM((half, width), F32),
+        pltpu.VMEM((half, width), BF),
+        pltpu.VMEM((half, width), BF),
+        pltpu.VMEM((1, width), F32),
+        pltpu.VMEM((N, tok, hf), BF),
+        pltpu.VMEM((N, tok, feats), BF),
+        sem((4,)),
+        sem((N,)), sem((N,)),
+        sem((2,)), sem((2,)),
+        sem((2, T)), sem((T,)),
+        sem((T,)), sem((2, T)),
+        sem((2, T)), sem((T,)),
+        sem((T,)), sem((2, T)),
+        sem((2, T)), sem((T,)),
+        sem((N, T)), sem((2, N, T)),
+        sem((N,)), sem((N,)),
+    ]
+    return pl.pallas_call(
+        functools.partial(kernel_pair, T, N),
+        out_shape=jax.ShapeDtypeStruct((feats, hf), F32),
+        in_specs=[vm(), vm(), vm(), hbm(), hbm(), hbm(), hbm()],
+        out_specs=vm(),
+        scratch_shapes=scratch,
+        compiler_params=pltpu.CompilerParams(
+            collective_id=0, has_side_effects=True, vmem_limit_bytes=56 * 1024 * 1024
+        ),
+    )(x, norm_gain, probs, w_val, w_dir, w_out, curvature)
+
+
 def per_device(section_input, norm_gain, value_weight, attn_probs, out_weight, direction, curvature):
     x = section_input[0]
     w_val = value_weight[0]
@@ -358,6 +661,8 @@
     rows = tok // T
     feats = width // N
     fused = feats % 128 == 0 and feats * N == width
+    if fused and S == 2 and rows % 32 == 0:
+        return call_pair(T, N, x, norm_gain, probs, w_val, w_dir, w_out, curvature)[None]
     vm = functools.partial(pl.BlockSpec, memory_space=pltpu.VMEM)
     hbm = functools.partial(pl.BlockSpec, memory_space=pl.ANY)
     if fused:

time: 129 us -> 99.3 us (0.77)
  the two profiles are of different devices: /device:TPU:23 before, /device:TPU:0 now
where the time goes in v2:
time: 99.3 us; the launch traced here: 99.1 us
  Pallas kernels  96.7 us (97%)
  local copies, waits for them, and re-layouts  2.36 us (2%)
    pallas_call x1, Pallas kernels, call_pair(): pl.pallas_call(functools.partial(kernel_pair, T, N), out_shape=jax.ShapeD...  96.7 us
    unnamed x1, local copies, waits for them, and re-layouts  2.36 us

profile of v2, /device:TPU:0, one launch (start us, length us, event | category | flops | bytes accessed | tf_op | source)
XLA Modules:
  0.0 99.1 jit_solution(11751701774662016762)
XLA Ops:
  0.0 96.7 %shard_map.73 = f32[768,384]{1,0:T(8,128)} custom-call(bf16[128,3072]{1,0:T(8,128)(2,1)} %bitcast.10, f32[1,3072]{1,0:T(1,128)} %gain_ref.1, bf16[3,128,128]{2,1,0:T(8,128)(2,1)} %bitcast.11, bf16[384,3072]{1,0:T(8,128)(2,1)} %bitcast.7, bf16[3072,384]{1,0:T(8,128)(2,1)} %bitcast.8, bf16[3072,384]{1,0:T(8,128)(2,1)} %bitcast.9, bf16[128,3072]{1,0:T(8,128)(2,1)} %curv_hbm.1), custom_call_target="tpu_custom_call" | custom-call | tf_op jit(solution)/shard_map/pallas_call | solution.py:638
  96.8 2.4 %copy.9 = f32[1,768,384]{2,1,0:T(8,128)} copy(f32[1,768,384]{2,1,0:T(8,128)} %bitcast.6) | data formatting | bytes 2359296

commit v3 on v2

--- a/solution.py
+++ b/solution.py
@@ -349,9 +349,9 @@
     x_ref, gain_ref, probs_ref, wv_hbm, wd_hbm, wo_hbm, curv_hbm,
     prod_ref,
     wv, wd, wo, curv, act, part, partb, in_a, in_d, in_f, gpartb, normed, tn, gfull, trow, xrow, grow,
-    gain1, actall, gall,
-    load_sem, act_send, act_recv, g_send, g_recv, a_send, a_recv, c_send, c_recv, d_send, d_recv,
-    e_send, e_recv, f_send, f_recv, h_send, h_recv, x_send, x_recv,
+    gain1, actall, gall, stage,
+    load_sem, act_send, act_recv, g_send, g_recv, a_send, a_recv, c_send, c_recv, c_relay, d_send, d_recv,
+    e_send, e_recv, e_relay, f_send, f_recv, h_send, h_recv, r_send, r_recv, x_send, x_recv,
 ):
     d = lax.axis_index("dp")
     s = lax.axis_index("section")
@@ -362,8 +362,12 @@
     heads = probs_ref.shape[0]
     hd = wv.shape[0] // heads
     feats = width // N
-    CH = 512 if width % 512 == 0 else width
-    chunks = [slice(c, c + CH) for c in range(0, width, CH)]
+    Q = 2
+    wide = width // Q
+    CH = 512 if wide % 512 == 0 else wide
+    cols = [slice(q * wide, (q + 1) * wide) for q in range(Q)]
+    parts = [[slice(c, c + CH) for c in range(q * wide, (q + 1) * wide, CH)] for q in range(Q)]
+    order = [k for k in range(1, T) if k in (1, T - 1)] + [k for k in range(2, T - 1)]
 
     def own(ss, jj):
         return pl.ds(pl.multiple_of(jj * rows + (1 - ss) * half, half), half)
@@ -423,37 +427,53 @@
 
     loads[1].wait()
 
-    def exchange(source, landing, send, recv, home, run):
+    def exchange(q, source, landing, send, recv, home, run):
+        c = cols[q]
         for ss in (1 - home, home):
             for k in range(T):
                 if ss == home and k == 0:
                     continue
                 j = peer(i, k, T)
-                run(remote(source.at[own(ss, j)], landing.at[k], send.at[ss, k], recv.at[k], at(d, ss, j)))
-
-    def collect(source, landing, send, recv, home, local):
+                run(remote(
+                    source.at[own(ss, j), c], landing.at[k, :, c], send.at[q, ss, k], recv.at[q, k], at(d, ss, j)
+                ))
+
+    def collect(q, source, landing, send, recv, local):
+        c = cols[q]
         first = 1 if local is not None else 0
         for k in range(first, T):
-            remote(source.at[own(s, i)], landing.at[k], send.at[0, k], recv.at[k], at(d, s, i)).wait_recv()
+            remote(
+                source.at[own(s, i), c], landing.at[k, :, c], send.at[q, 0, k], recv.at[q, k], at(d, s, i)
+            ).wait_recv()
         total = local
         for k in range(first, T):
-            piece = landing[k].astype(F32)
+            piece = landing[k, :, c].astype(F32)
             total = piece if total is None else total + piece
         return total
 
-    def spread_rows(buf, send, recv, me, run):
-        for k in range(T):
-            if me == 1 and k == 0:
-                continue
-            run(remote(buf.at[own(me, i)], buf.at[own(me, i)], send.at[k], recv.at[me, k], at(d, 1, peer(i, k, T))))
-
-    def gather_rows(buf, send, recv):
+    def spread_rows(q, buf, send, recv, relay, me, run):
+        r = own(me, i)
+        src = buf.at[r, cols[q]]
+        if me == 0:
+            run(remote(src, src, send.at[q, 0, 0], recv.at[q, 0, 0], at(d, 1, i)))
+        for k in range(1, T):
+            land = recv.at[q, 1, k] if me == 1 else relay.at[q, k]
+            run(remote(src, src, send.at[q, 0, k], land, at(d, me, peer(i, k, T))))
+
+    def pass_on(q, buf, send, recv, relay, run, wait):
+        for k in order:
+            src = buf.at[own(0, peer(i, T - k, T)), cols[q]]
+            if wait:
+                remote(src, src, send.at[q, 0, k], relay.at[q, k], at(d, s, i)).wait_recv()
+            run(remote(src, src, send.at[q, 1, k], recv.at[q, 0, k], at(d, 1, i)))
+
+    def gather_rows(q, buf, send, recv):
         for ss in (1, 0):
             for k in range(T):
                 if ss == 1 and k == 0:
                     continue
-                src = own(ss, peer(i, T - k, T))
-                remote(buf.at[src], buf.at[src], send.at[k], recv.at[ss, k], at(d, s, i)).wait_recv()
+                src = buf.at[own(ss, peer(i, T - k, T)), cols[q]]
+                remote(src, src, send.at[q, 0, k], recv.at[q, ss, k], at(d, s, i)).wait_recv()
 
     def start(copy):
         copy.start()
@@ -469,9 +489,10 @@
             gn * (rr * tb - rr**3 * xr * jnp.mean(xr * tb, axis=-1, keepdims=True))
         ).astype(BF)
 
-    def seed_rows(total):
-        tb = (total + trow[...]).astype(BF).astype(F32)
-        gfull[own(s, i)] = (curv[own(s, i)].astype(F32) * tb).astype(BF)
+    def seed_rows(q, total):
+        c = cols[q]
+        tb = (total + trow[:, c]).astype(BF).astype(F32)
+        gfull[own(s, i), c] = (curv[own(s, i), c].astype(F32) * tb).astype(BF)
 
     def adjoint_rows(total, xr, gn):
         rr = lax.rsqrt(jnp.mean(xr * xr, axis=-1, keepdims=True) + 1e-06)
@@ -480,23 +501,42 @@
         grow[...] = (gfull[own(s, i)].astype(F32) + gx).astype(BF)
 
     def hand_over(me, run):
-        for k in range(N):
-            for j in range(T):
+        for j in [0] + order if me == 1 else order + [0]:
+            for k in range(N):
                 if me == 0 and k == 0 and j == 0:
                     continue
                 dd = peer(d, k, N)
+                src = grow.at[:, feats_at(dd)]
+                if me == 1 and j > 0:
+                    run(remote(src, stage.at[k, j], h_send.at[k, j], r_recv.at[k, j], at(dd, 1, peer(i, j, T))))
+                else:
+                    run(remote(
+                        src, gall.at[d, own(me, i)], h_send.at[k, j], h_recv.at[me, k, j], at(dd, 0, peer(i, j, T))
+                    ))
+
+    def hand_on(run, wait):
+        for j in order:
+            for k in range(N):
+                if wait:
+                    remote(
+                        grow.at[:, feats_at(d)], stage.at[k, j], h_send.at[k, j], r_recv.at[k, j], at(d, s, i)
+                    ).wait_recv()
                 run(remote(
-                    grow.at[:, feats_at(dd)], gall.at[d, own(me, i)],
-                    h_send.at[k, j], h_recv.at[me, k, j], at(dd, 0, peer(i, j, T)),
+                    stage.at[k, j], gall.at[peer(d, N - k, N), own(1, peer(i, T - j, T))],
+                    r_send.at[k, j], h_recv.at[1, k, j], at(d, 0, i),
                 ))
+
+    def whole(sums):
+        return jnp.concatenate(sums, axis=1)
 
     @pl.when(s == 0)
     def _():
-        for c in chunks:
-            base = dot_nt(act[...], wd[c, :])
-            part[:, c] = base
-            partb[:, c] = base.astype(BF)
-        exchange(partb, in_a, a_send, a_recv, 0, start)
+        for q in range(Q):
+            for c in parts[q]:
+                base = dot_nt(act[...], wd[c, :])
+                part[:, c] = base
+                partb[:, c] = base.astype(BF)
+            exchange(q, partb, in_a, a_send, a_recv, 0, start)
         for k in range(1, N):
             copy_act(k, d).start()
         actall[d] = act[...]
@@ -504,13 +544,21 @@
             copy.wait_recv()
         xr = xrow[...].astype(F32)
         gn = gain1[...]
-        tangent_rows(collect(partb, in_a, a_send, a_recv, 0, part[own(0, i)]), xr, gn)
-        spread_rows(tn, c_send, c_recv, 0, start)
+        tangent_rows(
+            whole([collect(q, partb, in_a, a_send, a_recv, part[own(0, i), cols[q]]) for q in range(Q)]), xr, gn
+        )
+        for q in range(Q):
+            spread_rows(q, tn, c_send, c_recv, c_relay, 0, start)
+        for q in range(Q):
+            pass_on(q, tn, c_send, c_recv, c_relay, start, True)
         loads[2].wait()
         loads[3].wait()
-        seed_rows(collect(partb, in_d, d_send, d_recv, 1, None))
-        spread_rows(gfull, e_send, e_recv, 0, start)
-        adjoint_rows(collect(gpartb, in_f, f_send, f_recv, 1, None), xr, gn)
+        for q in range(Q):
+            seed_rows(q, collect(q, partb, in_d, d_send, d_recv, None))
+            spread_rows(q, gfull, e_send, e_recv, e_relay, 0, start)
+        for q in range(Q):
+            pass_on(q, gfull, e_send, e_recv, e_relay, start, True)
+        adjoint_rows(whole([collect(q, gpartb, in_f, f_send, f_recv, None) for q in range(Q)]), xr, gn)
         hand_over(0, start)
         gall[d, own(0, i)] = grow[:, feats_at(d)]
         for k in range(1, N):
@@ -525,9 +573,12 @@
                         gall.at[peer(d, N - k, N), own(ss, peer(i, T - j, T))],
                         h_send.at[k, j], h_recv.at[ss, k, j], at(d, s, i),
                     ).wait_recv()
-        exchange(partb, in_a, a_send, a_recv, 0, ended)
-        spread_rows(tn, c_send, c_recv, 0, ended)
-        spread_rows(gfull, e_send, e_recv, 0, ended)
+        for q in range(Q):
+            exchange(q, partb, in_a, a_send, a_recv, 0, ended)
+            spread_rows(q, tn, c_send, c_recv, c_relay, 0, ended)
+            pass_on(q, tn, c_send, c_recv, c_relay, ended, False)
+            spread_rows(q, gfull, e_send, e_recv, e_relay, 0, ended)
+            pass_on(q, gfull, e_send, e_recv, e_relay, ended, False)
         hand_over(0, ended)
 
     @pl.when(s == 1)
@@ -537,32 +588,45 @@
         for k in range(1, N):
             copy_act(k, d).start()
         actall[d] = act[...]
-        for c in chunks:
-            part[:, c] = dot_nt(act[...], wd[c, :])
+        for q in range(Q):
+            for c in parts[q]:
+                part[:, c] = dot_nt(act[...], wd[c, :])
         loads[2].wait()
         loads[3].wait()
         xr = x_ref[own(1, i)].astype(F32)
-        tangent_rows(collect(partb, in_a, a_send, a_recv, 0, None), xr, gain)
-        spread_rows(tn, c_send, c_recv, 1, start)
-        gather_rows(tn, c_send, c_recv)
-        tmix = mix(dot_nt(tn[...], wv[...]).astype(BF)).astype(BF)
-        for c in chunks:
-            more = part[:, c] + dot_nt(tmix, wo[c, :])
-            part[:, c] = more
-            partb[:, c] = more.astype(BF)
-        exchange(partb, in_d, d_send, d_recv, 1, start)
-        seed_rows(collect(partb, in_d, d_send, d_recv, 1, part[own(1, i)]))
-        spread_rows(gfull, e_send, e_recv, 1, start)
-        gather_rows(gfull, e_send, e_recv)
-        gm = dot_nn(gfull[...], wo[...]).astype(BF)
+        tangent_rows(whole([collect(q, partb, in_a, a_send, a_recv, None) for q in range(Q)]), xr, gain)
+        for q in range(Q):
+            spread_rows(q, tn, c_send, c_recv, None, 1, start)
+        tv = None
+        for q in range(Q):
+            gather_rows(q, tn, c_send, c_recv)
+            more = dot_nt(tn[:, cols[q]], wv[:, cols[q]])
+            tv = more if tv is None else tv + more
+        tmix = mix(tv.astype(BF)).astype(BF)
+        for q in range(Q):
+            for c in parts[q]:
+                more = part[:, c] + dot_nt(tmix, wo[c, :])
+                part[:, c] = more
+                partb[:, c] = more.astype(BF)
+            exchange(q, partb, in_d, d_send, d_recv, 1, start)
+        for q in range(Q):
+            seed_rows(q, collect(q, partb, in_d, d_send, d_recv, part[own(1, i), cols[q]]))
+            spread_rows(q, gfull, e_send, e_recv, None, 1, start)
+        gm = None
+        for q in range(Q):
+            gather_rows(q, gfull, e_send, e_recv)
+            more = dot_nn(gfull[:, cols[q]], wo[cols[q], :])
+            gm = more if gm is None else gm + more
+        gm = gm.astype(BF)
         gv = jnp.concatenate(
             [dot_tn(probs_ref[h], gm[:, h * hd : (h + 1) * hd]) for h in range(heads)], axis=1
         ).astype(BF)
-        for c in chunks:
-            gc = dot_nn(gv, wv[:, c])
-            part[:, c] = gc
-            gpartb[:, c] = gc.astype(BF)
-        exchange(gpartb, in_f, f_send, f_recv, 1, start)
+        for q in range(Q):
+            for c in parts[q]:
+                gc = dot_nn(gv, wv[:, c])
+                part[:, c] = gc
+                gpartb[:, c] = gc.astype(BF)
+            exchange(q, gpartb, in_f, f_send, f_recv, 1, start)
 
         def copy_x(k):
             dd = peer(d, k, N)
@@ -570,8 +634,11 @@
 
         for k in range(1, N):
             copy_x(k).start()
-        adjoint_rows(collect(gpartb, in_f, f_send, f_recv, 1, part[own(1, i)]), xr, gain)
+        adjoint_rows(
+            whole([collect(q, gpartb, in_f, f_send, f_recv, part[own(1, i), cols[q]]) for q in range(Q)]), xr, gain
+        )
         hand_over(1, start)
+        hand_on(start, True)
         gall[d] = gfull[:, feats_at(d)]
         for k in range(1, N):
             copy_act(k, peer(d, N - k, N)).wait_recv()
@@ -582,11 +649,13 @@
             copy.wait_send()
         for k in range(1, N):
             copy_x(k).wait_send()
-        spread_rows(tn, c_send, c_recv, 1, ended)
-        exchange(partb, in_d, d_send, d_recv, 1, ended)
-        spread_rows(gfull, e_send, e_recv, 1, ended)
-        exchange(gpartb, in_f, f_send, f_recv, 1, ended)
+        for q in range(Q):
+            spread_rows(q, tn, c_send, c_recv, None, 1, ended)
+            exchange(q, partb, in_d, d_send, d_recv, 1, ended)
+            spread_rows(q, gfull, e_send, e_recv, None, 1, ended)
+            exchange(q, gpartb, in_f, f_send, f_recv, 1, ended)
         hand_over(1, ended)
+        hand_on(ended, False)
 
     prod_ref[...] = dot_tn(
         gall[...].reshape(N * tok, feats), actall[...].reshape(N * tok, act.shape[1])
@@ -624,15 +693,16 @@
         pltpu.VMEM((1, width), F32),
         pltpu.VMEM((N, tok, hf), BF),
         pltpu.VMEM((N, tok, feats), BF),
+        pltpu.VMEM((N, T, half, feats), BF),
         sem((4,)),
         sem((N,)), sem((N,)),
         sem((2,)), sem((2,)),
-        sem((2, T)), sem((T,)),
-        sem((T,)), sem((2, T)),
-        sem((2, T)), sem((T,)),
-        sem((T,)), sem((2, T)),
-        sem((2, T)), sem((T,)),
-        sem((N, T)), sem((2, N, T)),
+        sem((2, 2, T)), sem((2, T)),
+        sem((2, 2, T)), sem((2, 2, T)), sem((2, T)),
+        sem((2, 2, T)), sem((2, T)),
+        sem((2, 2, T)), sem((2, 2, T)), sem((2, T)),
+        sem((2, 2, T)), sem((2, T)),
+        sem((N, T)), sem((2, N, T)), sem((N, T)), sem((N, T)),
         sem((N,)), sem((N,)),
     ]
     return pl.pallas_call(
@@ -661,7 +731,7 @@
     rows = tok // T
     feats = width // N
     fused = feats % 128 == 0 and feats * N == width
-    if fused and S == 2 and rows % 32 == 0:
+    if fused and S == 2 and rows % 32 == 0 and width % 256 == 0:
         return call_pair(T, N, x, norm_gain, probs, w_val, w_dir, w_out, curvature)[None]
     vm = functools.partial(pl.BlockSpec, memory_space=pltpu.VMEM)
     hbm = functools.partial(pl.BlockSpec, memory_space=pl.ANY)

time: 99.3 us -> 112 us (1.13)
  Pallas kernels: 96.7 us -> 110 us
    pallas_call x1, Pallas kernels: 96.7 us -> 110 us  [call_pair(): pl.pallas_call(functools.partial(kernel_pair, T, N), out_shape=jax.ShapeD...]
where the time goes in v3:
time: 112 us
  Pallas kernels  110 us (98%)
  local copies, waits for them, and re-layouts  2.36 us (2%)
    pallas_call x1, Pallas kernels, call_pair(): pl.pallas_call(functools.partial(kernel_pair, T, N), out_shape=jax.ShapeD...  110 us
    unnamed x1, local copies, waits for them, and re-layouts  2.36 us

profile of v3, /device:TPU:0, one launch (start us, length us, event | category | flops | bytes accessed | tf_op | source)
XLA Modules:
  0.0 112.0 jit_solution(9531636432828860935)
XLA Ops:
  0.0 109.7 %shard_map.73 = f32[768,384]{1,0:T(8,128)} custom-call(bf16[128,3072]{1,0:T(8,128)(2,1)} %bitcast.10, f32[1,3072]{1,0:T(1,128)} %gain_ref.1, bf16[3,128,128]{2,1,0:T(8,128)(2,1)} %bitcast.11, bf16[384,3072]{1,0:T(8,128)(2,1)} %bitcast.7, bf16[3072,384]{1,0:T(8,128)(2,1)} %bitcast.8, bf16[3072,384]{1,0:T(8,128)(2,1)} %bitcast.9, bf16[128,3072]{1,0:T(8,128)(2,1)} %curv_hbm.1), custom_call_target="tpu_custom_call" | custom-call | tf_op jit(solution)/shard_map/pallas_call | solution.py:708
  109.7 2.4 %copy.9 = f32[1,768,384]{2,1,0:T(8,128)} copy(f32[1,768,384]{2,1,0:T(8,128)} %bitcast.6) | data formatting | bytes 2359296

commit v4 on v3

--- a/solution.py
+++ b/solution.py
@@ -10,6 +10,10 @@
 MESH = pl.DeviceIdType.MESH
 BF = jnp.bfloat16
 F32 = jnp.float32
+HALVES = 2
+RELAY_ROWS = False
+RELAY_SUMS = True
+RELAY_ADJ = False
 
 
 def dot_nt(a, b):
@@ -349,10 +353,12 @@
     x_ref, gain_ref, probs_ref, wv_hbm, wd_hbm, wo_hbm, curv_hbm,
     prod_ref,
     wv, wd, wo, curv, act, part, partb, in_a, in_d, in_f, gpartb, normed, tn, gfull, trow, xrow, grow,
-    gain1, actall, gall, stage,
+    gain1, actall, gall, stage, hop1_buf, hop2_buf,
     load_sem, act_send, act_recv, g_send, g_recv, a_send, a_recv, c_send, c_recv, c_relay, d_send, d_recv,
-    e_send, e_recv, e_relay, f_send, f_recv, h_send, h_recv, r_send, r_recv, x_send, x_recv,
+    e_send, e_recv, e_relay, f_send, f_recv, h_send, h_recv, r_send, r_recv, x_send, x_recv, hop_send, hop_recv,
 ):
+    hop1 = (hop1_buf, hop_send.at[0], hop_recv.at[0])
+    hop2 = (hop2_buf, hop_send.at[1], hop_recv.at[1])
     d = lax.axis_index("dp")
     s = lax.axis_index("section")
     i = lax.axis_index("tensor")
@@ -362,7 +368,7 @@
     heads = probs_ref.shape[0]
     hd = wv.shape[0] // heads
     feats = width // N
-    Q = 2
+    Q = HALVES
     wide = width // Q
     CH = 512 if wide % 512 == 0 else wide
     cols = [slice(q * wide, (q + 1) * wide) for q in range(Q)]
@@ -427,16 +433,26 @@
 
     loads[1].wait()
 
-    def exchange(q, source, landing, send, recv, home, run):
+    def exchange(q, source, landing, send, recv, hop, home, run):
         c = cols[q]
         for ss in (1 - home, home):
             for k in range(T):
                 if ss == home and k == 0:
                     continue
                 j = peer(i, k, T)
-                run(remote(
-                    source.at[own(ss, j), c], landing.at[k, :, c], send.at[q, ss, k], recv.at[q, k], at(d, ss, j)
-                ))
+                src = source.at[own(ss, j), c]
+                if RELAY_SUMS and ss != home and k > 0:
+                    run(remote(src, hop[0].at[k, :, c], send.at[q, ss, k], hop[2].at[q, k], at(d, ss, i)))
+                else:
+                    run(remote(src, landing.at[k, :, c], send.at[q, ss, k], recv.at[q, k], at(d, ss, j)))
+
+    def forward(q, landing, recv, hop, run, wait):
+        c = cols[q]
+        for k in order if RELAY_SUMS else []:
+            src = hop[0].at[k, :, c]
+            if wait:
+                remote(src, src, hop[1].at[q, k], hop[2].at[q, k], at(d, s, i)).wait_recv()
+            run(remote(src, landing.at[k, :, c], hop[1].at[q, k], recv.at[q, k], at(d, s, peer(i, k, T))))
 
     def collect(q, source, landing, send, recv, local):
         c = cols[q]
@@ -457,11 +473,16 @@
         if me == 0:
             run(remote(src, src, send.at[q, 0, 0], recv.at[q, 0, 0], at(d, 1, i)))
         for k in range(1, T):
-            land = recv.at[q, 1, k] if me == 1 else relay.at[q, k]
-            run(remote(src, src, send.at[q, 0, k], land, at(d, me, peer(i, k, T))))
+            if me == 1:
+                land, where = recv.at[q, 1, k], 1
+            elif RELAY_ROWS:
+                land, where = relay.at[q, k], 0
+            else:
+                land, where = recv.at[q, 0, k], 1
+            run(remote(src, src, send.at[q, 0, k], land, at(d, where, peer(i, k, T))))
 
     def pass_on(q, buf, send, recv, relay, run, wait):
-        for k in order:
+        for k in order if RELAY_ROWS else []:
             src = buf.at[own(0, peer(i, T - k, T)), cols[q]]
             if wait:
                 remote(src, src, send.at[q, 0, k], relay.at[q, k], at(d, s, i)).wait_recv()
@@ -507,7 +528,7 @@
                     continue
                 dd = peer(d, k, N)
                 src = grow.at[:, feats_at(dd)]
-                if me == 1 and j > 0:
+                if RELAY_ADJ and me == 1 and j > 0:
                     run(remote(src, stage.at[k, j], h_send.at[k, j], r_recv.at[k, j], at(dd, 1, peer(i, j, T))))
                 else:
                     run(remote(
@@ -515,7 +536,7 @@
                     ))
 
     def hand_on(run, wait):
-        for j in order:
+        for j in order if RELAY_ADJ else []:
             for k in range(N):
                 if wait:
                     remote(
@@ -536,7 +557,7 @@
                 base = dot_nt(act[...], wd[c, :])
                 part[:, c] = base
                 partb[:, c] = base.astype(BF)
-            exchange(q, partb, in_a, a_send, a_recv, 0, start)
+            exchange(q, partb, in_a, a_send, a_recv, hop1, 0, start)
         for k in range(1, N):
             copy_act(k, d).start()
         actall[d] = act[...]
@@ -554,10 +575,14 @@
         loads[2].wait()
         loads[3].wait()
         for q in range(Q):
+            forward(q, in_d, d_recv, hop1, start, True)
+        for q in range(Q):
             seed_rows(q, collect(q, partb, in_d, d_send, d_recv, None))
             spread_rows(q, gfull, e_send, e_recv, e_relay, 0, start)
         for q in range(Q):
             pass_on(q, gfull, e_send, e_recv, e_relay, start, True)
+        for q in range(Q):
+            forward(q, in_f, f_recv, hop2, start, True)
         adjoint_rows(whole([collect(q, gpartb, in_f, f_send, f_recv, None) for q in range(Q)]), xr, gn)
         hand_over(0, start)
         gall[d, own(0, i)] = grow[:, feats_at(d)]
@@ -574,11 +599,14 @@
                         h_send.at[k, j], h_recv.at[ss, k, j], at(d, s, i),
                     ).wait_recv()
         for q in range(Q):
-            exchange(q, partb, in_a, a_send, a_recv, 0, ended)
+            exchange(q, partb, in_a, a_send, a_recv, hop1, 0, ended)
             spread_rows(q, tn, c_send, c_recv, c_relay, 0, ended)
             pass_on(q, tn, c_send, c_recv, c_relay, ended, False)
             spread_rows(q, gfull, e_send, e_recv, e_relay, 0, ended)
             pass_on(q, gfull, e_send, e_recv, e_relay, ended, False)
+        for q in range(Q):
+            forward(q, in_d, d_recv, hop1, ended, False)
+            forward(q, in_f, f_recv, hop2, ended, False)
         hand_over(0, ended)
 
     @pl.when(s == 1)
@@ -594,6 +622,8 @@
         loads[2].wait()
         loads[3].wait()
         xr = x_ref[own(1, i)].astype(F32)
+        for q in range(Q):
+            forward(q, in_a, a_recv, hop1, start, True)
         tangent_rows(whole([collect(q, partb, in_a, a_send, a_recv, None) for q in range(Q)]), xr, gain)
         for q in range(Q):
             spread_rows(q, tn, c_send, c_recv, None, 1, start)
@@ -608,7 +638,7 @@
                 more = part[:, c] + dot_nt(tmix, wo[c, :])
                 part[:, c] = more
                 partb[:, c] = more.astype(BF)
-            exchange(q, partb, in_d, d_send, d_recv, 1, start)
+            exchange(q, partb, in_d, d_send, d_recv, hop1, 1, start)
         for q in range(Q):
             seed_rows(q, collect(q, partb, in_d, d_send, d_recv, part[own(1, i), cols[q]]))
             spread_rows(q, gfull, e_send, e_recv, None, 1, start)
@@ -626,7 +656,7 @@
                 gc = dot_nn(gv, wv[:, c])
                 part[:, c] = gc
                 gpartb[:, c] = gc.astype(BF)
-            exchange(q, gpartb, in_f, f_send, f_recv, 1, start)
+            exchange(q, gpartb, in_f, f_send, f_recv, hop2, 1, start)
 
         def copy_x(k):
             dd = peer(d, k, N)
@@ -651,9 +681,11 @@
             copy_x(k).wait_send()
         for q in range(Q):
             spread_rows(q, tn, c_send, c_recv, None, 1, ended)
-            exchange(q, partb, in_d, d_send, d_recv, 1, ended)
+            exchange(q, partb, in_d, d_send, d_recv, hop1, 1, ended)
             spread_rows(q, gfull, e_send, e_recv, None, 1, ended)
-            exchange(q, gpartb, in_f, f_send, f_recv, 1, ended)
+            exchange(q, gpartb, in_f, f_send, f_recv, hop2, 1, ended)
+        for q in range(Q):
+            forward(q, in_a, a_recv, hop1, ended, False)
         hand_over(1, ended)
         hand_on(ended, False)
 
@@ -694,6 +726,8 @@
         pltpu.VMEM((N, tok, hf), BF),
         pltpu.VMEM((N, tok, feats), BF),
         pltpu.VMEM((N, T, half, feats), BF),
+        pltpu.VMEM((T, half, width), BF),
+        pltpu.VMEM((T, half, width), BF),
         sem((4,)),
         sem((N,)), sem((N,)),
         sem((2,)), sem((2,)),
@@ -704,6 +738,7 @@
         sem((2, 2, T)), sem((2, T)),
         sem((N, T)), sem((2, N, T)), sem((N, T)), sem((N, T)),
         sem((N,)), sem((N,)),
+        sem((2, 2, T)), sem((2, 2, T)),
     ]
     return pl.pallas_call(
         functools.partial(kernel_pair, T, N),

time: 112 us -> 91.3 us (0.82)
  Pallas kernels: 110 us -> 88.7 us
    pallas_call x1, Pallas kernels: 110 us -> 88.7 us  [call_pair(): pl.pallas_call(functools.partial(kernel_pair, T, N), out_shape=jax.ShapeD...]
where the time goes in v4:
time: 91.3 us; the launch traced here: 91.1 us
  Pallas kernels  88.7 us (97%)
  local copies, waits for them, and re-layouts  2.36 us (3%)
    pallas_call x1, Pallas kernels, call_pair(): pl.pallas_call(functools.partial(kernel_pair, T, N), out_shape=jax.ShapeD...  88.7 us
    unnamed x1, local copies, waits for them, and re-layouts  2.36 us

profile of v4, /device:TPU:0, one launch (start us, length us, event | category | flops | bytes accessed | tf_op | source)
XLA Modules:
  0.0 91.1 jit_solution(13611782297476483016)
XLA Ops:
  0.0 88.7 %shard_map.73 = f32[768,384]{1,0:T(8,128)} custom-call(bf16[128,3072]{1,0:T(8,128)(2,1)} %bitcast.10, f32[1,3072]{1,0:T(1,128)} %gain_ref.1, bf16[3,128,128]{2,1,0:T(8,128)(2,1)} %bitcast.11, bf16[384,3072]{1,0:T(8,128)(2,1)} %bitcast.7, bf16[3072,384]{1,0:T(8,128)(2,1)} %bitcast.8, bf16[3072,384]{1,0:T(8,128)(2,1)} %bitcast.9, bf16[128,3072]{1,0:T(8,128)(2,1)} %curv_hbm.1), custom_call_target="tpu_custom_call" | custom-call | tf_op jit(solution)/shard_map/pallas_call | solution.py:743
  88.7 2.4 %copy.9 = f32[1,768,384]{2,1,0:T(8,128)} copy(f32[1,768,384]{2,1,0:T(8,128)} %bitcast.6) | data formatting | bytes 2359296
